TPU v7x, 128 devices: a whole 4x4x4 slice. The times are simulated.
128 devices in a mesh: vel: 4 (over y_lo, core), pos: 32 (over y_hi, z, x).
Axes of the slice: x: 4, y: 4 (y_hi: 2, y_lo: 2; y = y_hi * 2 + y_lo), z: 4, core: 2. Of those that a mesh axis runs over, the one named last changes fastest.
Arguments:
- value_next: float32 [64, 64, 64, 512], P('pos', 'vel'), may hold values from -6 to 6
- density: float32 [64, 64, 64, 512], P('pos', 'vel'), as said below
Outputs:
- value_now: float32 [64, 64, 64, 512], P('pos', 'vel')
- density_next: float32 [64, 64, 64, 512], P('pos', 'vel')
Inputs may be any that keep to these rules, and one draw needn't show every extreme that they name: density is positive everywhere.
All inputs are finite; a program needn't handle non-finite values.
Results may differ from a plain program's by a relative error of at most 0.00002.
Values sent between devices are 32-bit elements; how exact they have to be, the bound alone decides.
A program may use at most 192 MiB of HBM per device.

v0:
```python
import jax
import jax.numpy as jnp
from jax import lax
from jax.sharding import PartitionSpec as P

COURANT = 0.4
CONTROL_COST = 0.25
VISCOSITY = 0.15
CROWDING = 0.3


def from_behind(block, axis, distance):
    devices = range(lax.axis_size(axis))
    route = [((i - distance) % len(devices), i) for i in devices]
    return lax.ppermute(block, axis, route)


def passed_along(value, axis, steps):
    count = lax.axis_size(axis)
    leading, last = (max(0, -steps), min(count, count - steps))
    return lax.ppermute(value, axis, [(source, source + steps) for source in range(leading, last)])


def speeds(first, count, total):
    index = first + jnp.arange(count, dtype=jnp.int32)
    return COURANT * ((index.astype(jnp.float32) + 0.5 - total / 2) / (total / 2))


def along_second(array, step):
    rolled = jnp.roll(array, -step, 2)
    place = lax.broadcasted_iota(jnp.int32, array.shape, 2)
    edge = array.shape[2] - 1 if step > 0 else 0
    return jnp.where(place == edge, array, rolled)


def value_core(centre, x_up, x_dn, a_up, a_dn, speed_x, speed_y, crowding):
    along_x = speed_x[None, :, None, None]
    along_y = speed_y[None, None, :, None]
    carry_x = jnp.where(along_x > 0, along_x * (x_up - centre), along_x * (centre - x_dn))
    ahead_y = jnp.roll(centre, -1, 3) - centre
    behind_y = centre - jnp.roll(centre, 1, 3)
    carry_y = jnp.where(along_y > 0, along_y * ahead_y, along_y * behind_y)
    upper_v = a_up - centre
    lower_v = centre - a_dn
    upper_w = along_second(centre, 1) - centre
    lower_w = centre - along_second(centre, -1)
    hamilton = 0.5 * (
        jnp.square(jnp.maximum(lower_v, 0.0))
        + jnp.square(jnp.minimum(upper_v, 0.0))
        + jnp.square(jnp.maximum(lower_w, 0.0))
        + jnp.square(jnp.minimum(upper_w, 0.0))
    )
    laplace = upper_v - lower_v + upper_w - lower_w
    return (
        centre
        + carry_x
        + carry_y
        - CONTROL_COST * hamilton
        + VISCOSITY * laplace
        + crowding[:, None, None, :]
    )


def density_core(centre, x_up, x_dn, a_up, a_dn, control, control_up, control_dn, speed_x, speed_y):
    along_x = speed_x[None, :, None, None]
    along_y = speed_y[None, None, :, None]
    carry_x = jnp.where(along_x > 0, along_x * (centre - x_dn), along_x * (x_up - centre))
    behind_y = centre - jnp.roll(centre, 1, 3)
    ahead_y = jnp.roll(centre, -1, 3) - centre
    carry_y = jnp.where(along_y > 0, along_y * behind_y, along_y * ahead_y)
    speed_up = -CONTROL_COST * (control_up - control)
    speed_dn = -CONTROL_COST * (control - control_dn)
    flux_up = jnp.maximum(speed_up, 0.0) * centre + jnp.minimum(speed_up, 0.0) * a_up
    flux_dn = jnp.maximum(speed_dn, 0.0) * a_dn + jnp.minimum(speed_dn, 0.0) * centre
    b_up = along_second(centre, 1)
    b_dn = along_second(centre, -1)
    side_up = -CONTROL_COST * (along_second(control, 1) - control)
    side_dn = -CONTROL_COST * (control - along_second(control, -1))
    flux_right = jnp.maximum(side_up, 0.0) * centre + jnp.minimum(side_up, 0.0) * b_up
    flux_left = jnp.maximum(side_dn, 0.0) * b_dn + jnp.minimum(side_dn, 0.0) * centre
    spread = VISCOSITY * (a_up + a_dn - 2.0 * centre + b_up + b_dn - 2.0 * centre)
    return centre - carry_x - carry_y - (flux_up - flux_dn) - (flux_right - flux_left) + spread


def velocity_rows(field, from_low, from_high, bottom, summit):
    lower = jnp.concatenate([jnp.where(bottom, field[:, :1], from_low), field[:, :-1]], 1)
    upper = jnp.concatenate([field[:, 1:], jnp.where(summit, field[:, -1:], from_high)], 1)
    return (upper, lower)


def body(value_next, density):
    row_count = value_next.shape[1]
    grid_v = value_next.shape[2]
    vel_place = lax.axis_index("vel")
    vel_count = lax.axis_size("vel")
    partial_mass = jnp.sum(density, axis=(1, 2))
    mass = lax.psum(partial_mass, "vel") / (grid_v * grid_v)
    crowding = CROWDING * mass * mass
    speed_y = speeds(0, grid_v, grid_v)
    speed_x = speeds(vel_place * row_count, row_count, grid_v)
    below_value, below_density = from_behind((value_next[-1:], density[-1:]), "pos", 1)
    above_value, above_density = from_behind((value_next[:1], density[:1]), "pos", -1)
    value_x_dn = jnp.concatenate([below_value, value_next[:-1]], 0)
    value_x_up = jnp.concatenate([value_next[1:], above_value], 0)
    density_x_dn = jnp.concatenate([below_density, density[:-1]], 0)
    density_x_up = jnp.concatenate([density[1:], above_density], 0)
    bottom = vel_place == 0
    summit = vel_place == vel_count - 1
    low_value, low_density = passed_along((value_next[:, -1:], density[:, -1:]), "vel", 1)
    high_value, high_density = passed_along((value_next[:, :1], density[:, :1]), "vel", -1)
    value_a_up, value_a_dn = velocity_rows(value_next, low_value, high_value, bottom, summit)
    density_a_up, density_a_dn = velocity_rows(density, low_density, high_density, bottom, summit)
    value_now = value_core(
        value_next, value_x_up, value_x_dn, value_a_up, value_a_dn, speed_x, speed_y, crowding
    )
    low_control = passed_along(value_now[:, -1:], "vel", 1)
    high_control = passed_along(value_now[:, :1], "vel", -1)
    control_up, control_dn = velocity_rows(value_now, low_control, high_control, bottom, summit)
    density_next = density_core(
        density,
        density_x_up,
        density_x_dn,
        density_a_up,
        density_a_dn,
        value_now,
        control_up,
        control_dn,
        speed_x,
        speed_y,
    )
    return (value_now, density_next)


def solution(mesh):
    placed = (P("pos", "vel", None, None), P("pos", "vel", None, None))
    return jax.shard_map(
        body,
        mesh=mesh,
        in_specs=placed,
        out_specs=(P("pos", "vel", None, None), P("pos", "vel", None, None)),
        check_vma=False,
    )
```

profile of v0, /device:TPU:7, one launch (start us, length us, event | category | flops | bytes accessed | tf_op | source)
XLA Modules:
  0.0 188.8 jit_solution(12290915281487704804)
XLA Ops:
  0.6 1.9 fusion.37
  2.5 3.8 %collective-permute-start.2 = (f32[2,1,64,512]{3,2,1,0:T(8,128)}, f32[2,1,64,512]{3,2,1,0:T(8,128)}, u32[]{:S(2)}, u32[]{:S(2)}) collective-permute-start(f32[2,1,64,512]{3,2,1,0:T(8,128)} %get-tuple-element.30), channel_id=1, source_target_pairs={{0,32},{32,64},{64,96},{1,33},{33,65},{65,97},{2,34},{34,66},{66,9... | collective-permute-start | bytes 786440 | tf_op jit(solution)/shard_map/ppermute | solution.py:21
  6.3 1.9 %collective-permute-start.3 = (f32[2,1,64,512]{3,2,1,0:T(8,128)}, f32[2,1,64,512]{3,2,1,0:T(8,128)}, u32[]{:S(2)}, u32[]{:S(2)}) collective-permute-start(f32[2,1,64,512]{3,2,1,0:T(8,128)} %get-tuple-element.31), channel_id=1, source_target_pairs={{32,0},{64,32},{96,64},{33,1},{65,33},{97,65},{34,2},{66,34},{98,6... | collective-permute-start | bytes 786440 | tf_op jit(solution)/shard_map/ppermute | solution.py:21
  8.2 1.9 %fusion.29 = (f32[2,1,64,512]{3,2,1,0:T(8,128)}, f32[2,1,64,512]{3,2,1,0:T(8,128)}) fusion(f32[2,16,64,512]{3,2,1,0:T(8,128)} %param.3), kind=kLoop, calls=%fused_computation.62 | loop fusion | bytes 1048576 | tf_op jit(solution)/shard_map/slice | solution.py:110
  10.1 2.3 %collective-permute-start.7 = (f32[2,1,64,512]{3,2,1,0:T(8,128)}, f32[2,1,64,512]{3,2,1,0:T(8,128)S(1)}, u32[]{:S(2)}, u32[]{:S(2)}) collective-permute-start(f32[2,1,64,512]{3,2,1,0:T(8,128)} %get-tuple-element.12), channel_id=1, source_target_pairs={{32,0},{64,32},{96,64},{33,1},{65,33},{97,65},{34,2},{66,34},{98,6... | collective-permute-start | bytes 786440 | tf_op jit(solution)/shard_map/ppermute | solution.py:21
  12.4 4.3 %fusion.43 = (f32[1,16,64,512]{3,2,1,0:T(8,128)S(1)}, f32[1,16,64,512]{3,2,1,0:T(8,128)}) fusion(f32[2,16,64,512]{3,2,1,0:T(8,128)} %param.2), kind=kLoop, calls=%fused_computation.76 | loop fusion | bytes 8388608 | tf_op jit(solution)/shard_map/slice | solution.py:104
  16.7 1.6 collective-permute-start.1
  18.3 0.0 collective-permute-start
  18.3 0.1 fusion.39
  18.4 0.8 fusion.33
  19.1 1.4 fusion.41
  20.6 1.7 fusion.35
  22.3 2.4 %fusion.36 = (f32[1,16,64,512]{3,2,1,0:T(8,128)}, f32[1,16,64,512]{3,2,1,0:T(8,128)}) fusion(f32[2,16,64,512]{3,2,1,0:T(8,128)S(1)} %copy-done), kind=kLoop, calls=%fused_computation.69 | loop fusion | bytes 8388608 | tf_op jit(solution)/shard_map/slice | solution.py:101
  24.7 4.1 %fusion.38 = (f32[2,15,64,512]{3,2,1,0:T(8,128)}, f32[2,15,64,512]{3,2,1,0:T(8,128)}) fusion(f32[2,16,64,512]{3,2,1,0:T(8,128)S(1)} %copy-done.3), kind=kLoop, calls=%fused_computation.71 | loop fusion | bytes 15728640 | tf_op jit(solution)/shard_map/slice | solution.py:86
  28.8 4.1 %fusion.28 = (f32[2,15,64,512]{3,2,1,0:T(8,128)}, f32[2,15,64,512]{3,2,1,0:T(8,128)}) fusion(f32[2,16,64,512]{3,2,1,0:T(8,128)S(1)} %copy-done), kind=kLoop, calls=%fused_computation.61 | loop fusion | bytes 15728640 | tf_op jit(solution)/shard_map/slice | solution.py:87
  32.9 4.9 %fusion.42 = (f32[2,16,64,511]{3,2,1,0:T(8,128)}, f32[2,16,64,511]{3,2,1,0:T(8,128)}) fusion(f32[2,16,64,512]{3,2,1,0:T(8,128)S(1)} %copy-done.3), kind=kLoop, calls=%fused_computation.75 | loop fusion | bytes 16744448 | tf_op jit(solution)/shard_map/jit(_roll_static)/slice | solution.py:41
  37.8 4.3 %fusion.40 = (f32[2,16,63,512]{3,2,1,0:T(8,128)}, f32[2,16,63,512]{3,2,1,0:T(8,128)}) fusion(f32[2,16,64,512]{3,2,1,0:T(8,128)S(1)} %copy-done.3), kind=kLoop, calls=%fused_computation.73 | loop fusion | bytes 16515072 | tf_op jit(solution)/shard_map/jit(_roll_static)/slice | solution.py:30
  42.0 2.5 %reduce_sum.9 = f32[2,512]{1,0:T(2,128)S(1)} reduce(f32[2,16,64,512]{3,2,1,0:T(8,128)} %param.3, f32[]{:T(128)} %constant.20.clone.1), dimensions={1,2}, to_apply=%region_0.0 | reduce | flops 1047552 | bytes 4198404 | tf_op jit(solution)/shard_map/reduce_sum | solution.py:96
  44.5 6.7 %psum.7 = f32[2,512]{1,0:T(2,128)S(1)} all-reduce(f32[2,512]{1,0:T(2,128)S(1)} %reduce_sum.9), channel_id=1, replica_groups=mesh['vel'=4,'pos'=32] {'vel'}, use_global_device_ids=true, to_apply=%region_1.0 | all-reduce | flops 1024 | bytes 8192 | tf_op jit(solution)/shard_map/psum | solution.py:97
  51.2 0.0 copy-start.1
  51.2 8.2 %fusion.34 = (f32[2,16,64,511]{3,2,1,0:T(8,128)}, f32[2,16,64,511]{3,2,1,0:T(8,128)}) fusion(f32[2,16,64,512]{3,2,1,0:T(8,128)} %param.3), kind=kLoop, calls=%fused_computation.67 | loop fusion | bytes 16744448 | tf_op jit(solution)/shard_map/jit(_roll_static)/slice | solution.py:69
  59.3 4.2 %fusion.32 = (f32[2,16,63,512]{3,2,1,0:T(8,128)}, f32[2,16,63,512]{3,2,1,0:T(8,128)}) fusion(f32[2,16,64,512]{3,2,1,0:T(8,128)S(1)} %copy-done.1), kind=kLoop, calls=%fused_computation.65 | loop fusion | bytes 16515072 | tf_op jit(solution)/shard_map/jit(_roll_static)/slice | solution.py:30
  63.5 0.6 iota_compare_fusion
  64.1 0.0 collective-permute-done.2
  64.1 23.2 %collective-permute-start.9 = (f32[2,1,64,512]{3,2,1,0:T(8,128)}, f32[2,1,64,512]{3,2,1,0:T(8,128)}, u32[]{:S(2)}, u32[]{:S(2)}) collective-permute-start(f32[2,1,64,512]{3,2,1,0:T(8,128)} %get-tuple-element.13), channel_id=1, source_target_pairs={{0,32},{32,64},{64,96},{1,33},{33,65},{65,97},{2,34},{34,66},{66,9... | collective-permute-start | bytes 786440 | tf_op jit(solution)/shard_map/ppermute | solution.py:21
  87.4 0.6 add_multiply_fusion
  88.0 0.0 collective-permute-done.3
  88.0 0.0 collective-permute-start.4
  88.0 1.3 broadcast_select_fusion.5
  89.2 0.0 collective-permute-done.7
  89.3 1.7 collective-permute-start.5
  91.0 40.7 %collective-permute-done.9 = f32[2,1,64,512]{3,2,1,0:T(8,128)} collective-permute-done((f32[2,1,64,512]{3,2,1,0:T(8,128)}, f32[2,1,64,512]{3,2,1,0:T(8,128)}, u32[]{:S(2)}, u32[]{:S(2)}) %collective-permute-start.9) | collective-permute-done | bytes 262176 | tf_op jit(solution)/shard_map/ppermute | solution.py:21
  131.7 2.0 %broadcast_select_fusion = (f32[2,1,64,512]{3,2,1,0:T(8,128)S(1)}, f32[2,1,64,512]{3,2,1,0:T(8,128)}) fusion(f32[2,1,64,512]{3,2,1,0:T(8,128)} %copy-done.10, pred[]{:T(512)S(6)} %eq.27, f32[2,16,64,512]{3,2,1,0:T(8,128)} %param.3, f32[2,1,64,512]{3,2,1,0:T(8,128)} %collective-permute-done.9, pred[]{:T(512)S(6)} %eq.26), kind=kLoop, calls=%fused_computation.46 | loop fusion | flops 131072 | bytes 1572866 | tf_op jit(solution)/shard_map/jit(_where)/select_n | solution.py:87
  133.7 0.0 collective-permute-done.1
  133.7 0.0 collective-permute-done
  133.7 13.8 %fusion.8 = f32[2,16,64,512]{3,2,1,0:T(8,128)S(1)} fusion(f32[2,16,64,512]{3,2,1,0:T(8,128)} %param.2, f32[1,16,64,512]{3,2,1,0:T(8,128)} %collective-permute-done, f32[1,16,64,512]{3,2,1,0:T(8,128)S(1)} %get-tuple-element.42, f32[1,16,64,512]{3,2,1,0:T(8,128)} %get-tuple-element.43, f32[1,16,64,512]{3,2,1,0:T(8,128)} %collective-permute-done.1, ...), kind=kLoop, calls=%fused_computation.13 | loop fusion | flops 47185920 | bytes 41947664 | tf_op jit(solution)/shard_map/add | solution.py:55
  147.5 0.0 copy-start.4
  147.5 0.9 fusion.27
  148.5 1.9 %collective-permute-start.6 = (f32[2,1,64,512]{3,2,1,0:T(8,128)}, f32[2,1,64,512]{3,2,1,0:T(8,128)}, u32[]{:S(2)}, u32[]{:S(2)}) collective-permute-start(f32[2,1,64,512]{3,2,1,0:T(8,128)} %get-tuple-element.6), channel_id=1, source_target_pairs={{32,0},{64,32},{96,64},{33,1},{65,33},{97,65},{34,2},{66,34},{98,6... | collective-permute-start | bytes 786440 | tf_op jit(solution)/shard_map/ppermute | solution.py:21
  150.4 4.4 %collective-permute-start.8 = (f32[2,1,64,512]{3,2,1,0:T(8,128)}, f32[2,1,64,512]{3,2,1,0:T(8,128)}, u32[]{:S(2)}, u32[]{:S(2)}) collective-permute-start(f32[2,1,64,512]{3,2,1,0:T(8,128)} %get-tuple-element.7), channel_id=1, source_target_pairs={{0,32},{32,64},{64,96},{1,33},{33,65},{65,97},{2,34},{34,66},{66,9... | collective-permute-start | bytes 786440 | tf_op jit(solution)/shard_map/ppermute | solution.py:21
  154.8 4.3 %fusion.30 = (f32[2,16,63,512]{3,2,1,0:T(8,128)}, f32[2,16,63,512]{3,2,1,0:T(8,128)}) fusion(f32[2,16,64,512]{3,2,1,0:T(8,128)S(1)} %fusion.8), kind=kLoop, calls=%fused_computation.63 | loop fusion | bytes 16515072 | tf_op jit(solution)/shard_map/jit(_roll_static)/slice | solution.py:30
  159.2 5.0 %fusion.26 = (f32[2,15,64,512]{3,2,1,0:T(8,128)}, f32[2,15,64,512]{3,2,1,0:T(8,128)}) fusion(f32[2,16,64,512]{3,2,1,0:T(8,128)S(1)} %fusion.8), kind=kLoop, calls=%fused_computation.59 | loop fusion | bytes 15728640 | tf_op jit(solution)/shard_map/slice | solution.py:87
  164.2 0.1 fusion.31
  164.4 1.9 %broadcast_select_fusion.1 = (f32[2,1,64,512]{3,2,1,0:T(8,128)S(1)}, f32[2,1,64,512]{3,2,1,0:T(8,128)S(1)}) fusion(f32[2,1,64,512]{3,2,1,0:T(8,128)} %collective-permute-done.6, pred[]{:T(512)S(6)} %eq.27, f32[2,16,64,512]{3,2,1,0:T(8,128)S(1)} %fusion.8, f32[2,1,64,512]{3,2,1,0:T(8,128)} %collective-permute-done.8, pred[]{:T(512)S(6)} %eq.26), kind=kLoop, calls=%fused_computation.47 | loop fusion | flops 131072 | bytes 1572866 | tf_op jit(solution)/shard_map/jit(_where)/select_n | solution.py:87
  166.3 0.0 collective-permute-done.5
  166.4 0.4 copy-done.6
  166.8 1.2 copy-done.7
  168.0 20.8 %fusion.19 = f32[2,16,64,512]{3,2,1,0:T(8,128)} fusion(f32[2,16,64,512]{3,2,1,0:T(8,128)S(1)} %copy-done.2, f32[1,16,64,512]{3,2,1,0:T(8,128)} %get-tuple-element.27, f32[1,16,64,512]{3,2,1,0:T(8,128)} %collective-permute-done.4, f32[1,16,64,512]{3,2,1,0:T(8,128)} %collective-permute-done.5, f32[1,16,64,512]{3,2,1,0:T(8,128)} %get-tuple-element.26, ...), kind=kLoop, calls=%fused_computation.30 | loop fusion | flops 71303168 | bytes 62915088 | tf_op jit(solution)/shard_map/add | solution.py:82
  (35 shorter events, 0.1 us)
Async XLA Ops:
  2.5 61.6 %collective-permute-start.2 = (f32[2,1,64,512]{3,2,1,0:T(8,128)}, f32[2,1,64,512]{3,2,1,0:T(8,128)}, u32[]{:S(2)}, u32[]{:S(2)}) collective-permute-start(f32[2,1,64,512]{3,2,1,0:T(8,128)} %get-tuple-element.30), channel_id=1, source_target_pairs={{0,32},{32,64},{64,96},{1,33},{33,65},{65,97},{2,34},{34,66},{66,9... | collective-permute-start | bytes 786440 | tf_op jit(solution)/shard_map/ppermute | solution.py:21
  6.3 81.7 %collective-permute-start.3 = (f32[2,1,64,512]{3,2,1,0:T(8,128)}, f32[2,1,64,512]{3,2,1,0:T(8,128)}, u32[]{:S(2)}, u32[]{:S(2)}) collective-permute-start(f32[2,1,64,512]{3,2,1,0:T(8,128)} %get-tuple-element.31), channel_id=1, source_target_pairs={{32,0},{64,32},{96,64},{33,1},{65,33},{97,65},{34,2},{66,34},{98,6... | collective-permute-start | bytes 786440 | tf_op jit(solution)/shard_map/ppermute | solution.py:21
  10.1 8.2 %copy-start.3 = (f32[2,16,64,512]{3,2,1,0:T(8,128)S(1)}, f32[2,16,64,512]{3,2,1,0:T(8,128)}, u32[]{:S(2)}) copy-start(f32[2,16,64,512]{3,2,1,0:T(8,128)} %param.2) | copy-start | bytes 12582916
  10.1 8.3 %copy-start = (f32[2,16,64,512]{3,2,1,0:T(8,128)S(1)}, f32[2,16,64,512]{3,2,1,0:T(8,128)}, u32[]{:S(2)}) copy-start(f32[2,16,64,512]{3,2,1,0:T(8,128)} %param.3) | copy-start | bytes 12582916
  10.1 79.1 %collective-permute-start.7 = (f32[2,1,64,512]{3,2,1,0:T(8,128)}, f32[2,1,64,512]{3,2,1,0:T(8,128)S(1)}, u32[]{:S(2)}, u32[]{:S(2)}) collective-permute-start(f32[2,1,64,512]{3,2,1,0:T(8,128)} %get-tuple-element.12), channel_id=1, source_target_pairs={{32,0},{64,32},{96,64},{33,1},{65,33},{97,65},{34,2},{66,34},{98,6... | collective-permute-start | bytes 786440 | tf_op jit(solution)/shard_map/ppermute | solution.py:21
  16.7 117.0 %collective-permute-start.1 = (f32[1,16,64,512]{3,2,1,0:T(8,128)S(1)}, f32[1,16,64,512]{3,2,1,0:T(8,128)}, u32[]{:S(2)}, u32[]{:S(2)}) collective-permute-start(f32[1,16,64,512]{3,2,1,0:T(8,128)S(1)} %get-tuple-element.42), channel_id=1, source_target_pairs={{31,0},{0,1},{1,2},{2,3},{3,4},{4,5},{5,6},{6,7},{7,8},{8,9},{9,10... | collective-permute-start | bytes 6291464 | tf_op jit(solution)/shard_map/ppermute | solution.py:15
  18.3 115.4 %collective-permute-start = (f32[1,16,64,512]{3,2,1,0:T(8,128)}, f32[1,16,64,512]{3,2,1,0:T(8,128)}, u32[]{:S(2)}, u32[]{:S(2)}) collective-permute-start(f32[1,16,64,512]{3,2,1,0:T(8,128)} %get-tuple-element.43), channel_id=1, source_target_pairs={{1,0},{2,1},{3,2},{4,3},{5,4},{6,5},{7,6},{8,7},{9,8},{10,9},{11,1... | collective-permute-start | bytes 6291464 | tf_op jit(solution)/shard_map/ppermute | solution.py:15
  51.2 8.2 %copy-start.1 = (f32[2,16,64,512]{3,2,1,0:T(8,128)S(1)}, f32[2,16,64,512]{3,2,1,0:T(8,128)}, u32[]{:S(2)}) copy-start(f32[2,16,64,512]{3,2,1,0:T(8,128)} %param.3) | copy-start | bytes 12582916
  64.1 67.6 %collective-permute-start.9 = (f32[2,1,64,512]{3,2,1,0:T(8,128)}, f32[2,1,64,512]{3,2,1,0:T(8,128)}, u32[]{:S(2)}, u32[]{:S(2)}) collective-permute-start(f32[2,1,64,512]{3,2,1,0:T(8,128)} %get-tuple-element.13), channel_id=1, source_target_pairs={{0,32},{32,64},{64,96},{1,33},{33,65},{65,97},{2,34},{34,66},{66,9... | collective-permute-start | bytes 786440 | tf_op jit(solution)/shard_map/ppermute | solution.py:21
  88.0 78.3 %collective-permute-start.4 = (f32[1,16,64,512]{3,2,1,0:T(8,128)}, f32[1,16,64,512]{3,2,1,0:T(8,128)}, u32[]{:S(2)}, u32[]{:S(2)}) collective-permute-start(f32[1,16,64,512]{3,2,1,0:T(8,128)} %get-tuple-element.26), channel_id=1, source_target_pairs={{31,0},{0,1},{1,2},{2,3},{3,4},{4,5},{5,6},{6,7},{7,8},{8,9},{9,10... | collective-permute-start | bytes 6291464 | tf_op jit(solution)/shard_map/ppermute | solution.py:15
  89.2 1.7 copy-start.10
  89.3 77.1 %collective-permute-start.5 = (f32[1,16,64,512]{3,2,1,0:T(8,128)}, f32[1,16,64,512]{3,2,1,0:T(8,128)}, u32[]{:S(2)}, u32[]{:S(2)}) collective-permute-start(f32[1,16,64,512]{3,2,1,0:T(8,128)} %get-tuple-element.27), channel_id=1, source_target_pairs={{1,0},{2,1},{3,2},{4,3},{5,4},{6,5},{7,6},{8,7},{9,8},{10,9},{11,1... | collective-permute-start | bytes 6291464 | tf_op jit(solution)/shard_map/ppermute | solution.py:15
  147.5 18.8 %copy-start.4 = (f32[2,16,64,512]{3,2,1,0:T(8,128)}, f32[2,16,64,512]{3,2,1,0:T(8,128)S(1)}, u32[]{:S(2)}) copy-start(f32[2,16,64,512]{3,2,1,0:T(8,128)S(1)} %fusion.8) | copy-start | bytes 12582916
  148.5 15.9 %collective-permute-start.6 = (f32[2,1,64,512]{3,2,1,0:T(8,128)}, f32[2,1,64,512]{3,2,1,0:T(8,128)}, u32[]{:S(2)}, u32[]{:S(2)}) collective-permute-start(f32[2,1,64,512]{3,2,1,0:T(8,128)} %get-tuple-element.6), channel_id=1, source_target_pairs={{32,0},{64,32},{96,64},{33,1},{65,33},{97,65},{34,2},{66,34},{98,6... | collective-permute-start | bytes 786440 | tf_op jit(solution)/shard_map/ppermute | solution.py:21
  150.4 14.0 %collective-permute-start.8 = (f32[2,1,64,512]{3,2,1,0:T(8,128)}, f32[2,1,64,512]{3,2,1,0:T(8,128)}, u32[]{:S(2)}, u32[]{:S(2)}) collective-permute-start(f32[2,1,64,512]{3,2,1,0:T(8,128)} %get-tuple-element.7), channel_id=1, source_target_pairs={{0,32},{32,64},{64,96},{1,33},{33,65},{65,97},{2,34},{34,66},{66,9... | collective-permute-start | bytes 786440 | tf_op jit(solution)/shard_map/ppermute | solution.py:21
  154.8 11.5 %copy-start.8 = (f32[2,16,64,1]{3,2,1,0:T(8,128)S(1)}, f32[2,16,64,1]{3,2,1,0:T(8,128)}, u32[]{:S(2)}) copy-start(f32[2,16,64,1]{3,2,1,0:T(8,128)} %get-tuple-element.24) | copy-start | bytes 24580
  159.1 7.2 %copy-start.2 = (f32[2,16,64,512]{3,2,1,0:T(8,128)S(1)}, f32[2,16,64,512]{3,2,1,0:T(8,128)}, u32[]{:S(2)}) copy-start(f32[2,16,64,512]{3,2,1,0:T(8,128)} %param.3) | copy-start | bytes 12582916
  159.1 7.2 %copy-start.5 = (f32[2,16,64,511]{3,2,1,0:T(8,128)S(1)}, f32[2,16,64,511]{3,2,1,0:T(8,128)}, u32[]{:S(2)}) copy-start(f32[2,16,64,511]{3,2,1,0:T(8,128)} %get-tuple-element.22) | copy-start | bytes 12558340
  159.1 7.7 %copy-start.6 = (f32[2,16,64,511]{3,2,1,0:T(8,128)S(1)}, f32[2,16,64,511]{3,2,1,0:T(8,128)}, u32[]{:S(2)}) copy-start(f32[2,16,64,511]{3,2,1,0:T(8,128)} %get-tuple-element.23) | copy-start | bytes 12558340
  159.1 8.8 %copy-start.7 = (f32[2,16,63,512]{3,2,1,0:T(8,128)S(1)}, f32[2,16,63,512]{3,2,1,0:T(8,128)}, u32[]{:S(2)}) copy-start(f32[2,16,63,512]{3,2,1,0:T(8,128)} %get-tuple-element.18) | copy-start | bytes 12386308
  159.1 8.8 %copy-start.9 = (f32[2,1,64,512]{3,2,1,0:T(8,128)S(1)}, f32[2,1,64,512]{3,2,1,0:T(8,128)}, u32[]{:S(2)}) copy-start(f32[2,1,64,512]{3,2,1,0:T(8,128)} %get-tuple-element.11) | copy-start | bytes 786436
  159.2 8.8 %copy-start.11 = (f32[2,16,1,512]{3,2,1,0:T(1,128)S(1)}, f32[2,16,1,512]{3,2,1,0:T(1,128)}, u32[]{:S(2)}) copy-start(f32[2,16,1,512]{3,2,1,0:T(1,128)} %get-tuple-element.20) | copy-start | bytes 196612
  159.2 8.8 %copy-start.12 = (f32[2,16,1,512]{3,2,1,0:T(1,128)S(1)}, f32[2,16,1,512]{3,2,1,0:T(1,128)}, u32[]{:S(2)}) copy-start(f32[2,16,1,512]{3,2,1,0:T(1,128)} %get-tuple-element.21) | copy-start | bytes 196612
  159.2 8.8 %copy-start.13 = (pred[64]{0:T(512)(128)(4,1)S(1)}, pred[64]{0:T(512)(128)(4,1)}, u32[]{:S(2)}) copy-start(pred[64]{0:T(512)(128)(4,1)} %get-tuple-element.44) | copy-start | bytes 196
  159.2 8.8 %copy-start.14 = (pred[64]{0:T(512)(128)(4,1)S(1)}, pred[64]{0:T(512)(128)(4,1)}, u32[]{:S(2)}) copy-start(pred[64]{0:T(512)(128)(4,1)} %get-tuple-element.45) | copy-start | bytes 196
  159.2 8.8 %copy-start.15 = (f32[64]{0:T(128)S(1)}, f32[64]{0:T(128)}, u32[]{:S(2)}) copy-start(f32[64]{0:T(128)} %add_multiply_fusion) | copy-start | bytes 772
where the time goes:
time: 189 us
  local copies, waits for them, and re-layouts  56.2 us (30%)
  other arithmetic  43.5 us (23%)
  starting transfers between devices  40.8 us (22%)
  waiting for transfers between devices  40.8 us (22%)
  blocking collectives  6.67 us (4%)
    ppermute x6, waiting for transfers between devices, passed_along(): lax.ppermute(value, axis, [(source, source + steps) for source in range(l...  40.7 us
    ppermute x6, starting transfers between devices, passed_along(): lax.ppermute(value, axis, [(source, source + steps) for source in range(l...  37.5 us
    add x1, other arithmetic, density_core(): centre - carry_x - carry_y - (flux_up - flux_dn) - (flux_right - flux_left)  20.8 us
    add x1, other arithmetic, value_core(): centre + carry_x + carry_y - CONTROL_COST * hamilton + VISCOSITY * laplace  13.8 us
    slice x6, local copies, waits for them, and re-layouts, along_second(): rolled = jnp.roll(array, -step, 2)  13.8 us
    slice x2, local copies, waits for them, and re-layouts, density_core(): ahead_y = jnp.roll(centre, -1, 3) - centre  9.87 us
    slice x2, local copies, waits for them, and re-layouts, velocity_rows(): field[:, 1:]  9.1 us
    psum x1, blocking collectives, body(): mass = lax.psum(partial_mass, 'vel') / (grid_v * grid_v)  6.67 us
  transfers between devices with their start and end apart: 10, of which 1 were waited for; matrix products, arithmetic and copies ran while one was open for 40% of the time, Pallas kernels for 0%

commit v1 on v0

v1 whole, which is shorter than its diff:
```python
import jax
import jax.numpy as jnp
from jax import lax
from jax.experimental import pallas as pl
from jax.experimental.pallas import tpu as pltpu
from jax.sharding import PartitionSpec as P

COURANT = 0.4
CONTROL_COST = 0.25
VISCOSITY = 0.15
CROWDING = 0.3
LANES = 128


def make_kernel(vels, slabs, rows, grid_v, cells, axes):
    blocks = cells // LANES
    half = grid_v // 2
    inner = rows - 1

    def device(vel, pos):
        place = {"vel": vel, "pos": pos}
        return tuple(place[name] for name in axes)

    def remote(src, dst, send, recv, target):
        return pltpu.make_async_remote_copy(
            src_ref=src,
            dst_ref=dst,
            send_sem=send,
            recv_sem=recv,
            device_id=target,
            device_id_type=pl.DeviceIdType.MESH,
        )

    def kernel(
        value, density, now, nxt,
        val, den, val_x, den_x, val_h, den_h, now_h, mass, crowd, slope,
        load_sem, x_send, x_recv, h_send, h_recv, n_send, n_recv, m_send, m_recv,
    ):
        vel = lax.axis_index("vel")
        pos = lax.axis_index("pos")
        rising = (vel >= vels // 2).astype(jnp.int32)
        after = lax.rem(pos + 1, slabs)
        before = lax.rem(pos + slabs - 1, slabs)
        val_to = jnp.where(rising == 1, before, after)
        den_to = jnp.where(rising == 1, after, before)
        near = 1 - rising
        far = rising

        load_den = pltpu.make_async_copy(density, den, load_sem.at[0])
        load_val = pltpu.make_async_copy(value, val, load_sem.at[1])
        load_den.start()
        load_val.start()

        barrier = pltpu.get_barrier_semaphore()
        pl.semaphore_signal(barrier, 1, device_id=device(vel, after), device_id_type=pl.DeviceIdType.MESH)
        pl.semaphore_signal(barrier, 1, device_id=device(vel, before), device_id_type=pl.DeviceIdType.MESH)
        for step in range(1, vels):
            pl.semaphore_signal(
                barrier, 1, device_id=device(lax.rem(vel + step, vels), pos),
                device_id_type=pl.DeviceIdType.MESH,
            )
        pl.semaphore_wait(barrier, vels + 1)

        def x_copies(a):
            return (
                remote(value.at[near, a], val_x.at[a], x_send.at[0, a], x_recv.at[0, a], device(vel, val_to)),
                remote(density.at[far, a], den_x.at[a], x_send.at[1, a], x_recv.at[1, a], device(vel, den_to)),
            )

        def start_x(a):
            for copy in x_copies(a):
                copy.start()

        start_x(0)
        start_x(rows - 1)

        upward = device(jnp.minimum(vel + 1, vels - 1), pos)
        downward = device(jnp.maximum(vel - 1, 0), pos)

        def h_copies(which):
            array, held = ((value, val_h), (density, den_h))[which]
            return (
                remote(array.at[:, rows - 1], held.at[0], h_send.at[which, 0], h_recv.at[which, 0], upward),
                remote(array.at[:, 0], held.at[1], h_send.at[which, 1], h_recv.at[which, 1], downward),
            )

        def start_middle(a, carry):
            start_x(a)
            return carry

        lax.fori_loop(1, rows - 1, start_middle, 0)

        index = lax.broadcasted_iota(jnp.int32, (grid_v, LANES), 0).astype(jnp.float32)
        slope[...] = jnp.abs(COURANT * ((index + 0.5 - grid_v / 2) / (grid_v / 2)))

        load_den.wait()
        for i in range(2):
            def add_row(a, total):
                row = den[i, a]
                for k in range(grid_v // 8):
                    total = total + row[8 * k:8 * k + 8]
                return total

            total = lax.fori_loop(0, rows, add_row, jnp.zeros((8, cells), jnp.float32))
            mass[vel, pl.ds(i, 1)] = jnp.sum(total, axis=0, keepdims=True)

        def m_copy(step):
            return remote(
                mass.at[vel], mass.at[vel], m_send.at[step - 1], m_recv.at[step - 1],
                device(lax.rem(vel + step, vels), pos),
            )

        for step in range(1, vels):
            m_copy(step).start()
        for which in (0, 1):
            up, down = h_copies(which)
            pl.when(vel < vels - 1)(up.start)
            pl.when(vel > 0)(down.start)
        load_val.wait()
        for step in range(1, vels):
            m_copy(step).wait_recv()
        for i in range(2):
            whole = mass[0, pl.ds(i, 1)]
            for group in range(1, vels):
                whole = whole + mass[group, pl.ds(i, 1)]
            whole = whole / (grid_v * grid_v)
            crowd[i] = jnp.broadcast_to(CROWDING * whole * whole, (8, cells))

        place_b = lax.broadcasted_iota(jnp.int32, (grid_v, LANES), 0)
        first_b = place_b == 0
        last_b = place_b == grid_v - 1
        lane = lax.broadcasted_iota(jnp.int32, (half, LANES), 1)

        def speed(a):
            place = (vel * rows + a).astype(jnp.float32)
            return jnp.abs(COURANT * ((place + 0.5 - grid_v / 2) / (grid_v / 2)))

        def cut(block):
            return pl.ds((block % blocks) * LANES, LANES)

        def shifted(ref, i, a, block, lower_step):
            def part(start, step):
                here = ref[i, a, pl.ds(start, half), cut(block)]
                there = ref[i, a, pl.ds(start, half), cut(block + step)]
                amount = LANES - 1 if step > 0 else 1
                edge = LANES - 1 if step > 0 else 0
                return jnp.where(lane == edge, pltpu.roll(there, amount, 1), pltpu.roll(here, amount, 1))

            return jnp.concatenate([part(0, lower_step), part(half, -lower_step)], 0)

        def value_row(i, a, x_row, up_row, down_row):
            pace = speed(a)
            for block in range(blocks):
                centre = val[i, a, :, cut(block)]
                upper = up_row(block, centre) - centre
                lower = centre - down_row(block, centre)
                side = jnp.where(last_b, 0.0, pltpu.roll(centre, grid_v - 1, 0) - centre)
                back = jnp.where(first_b, 0.0, pltpu.roll(side, 1, 0))
                bend = (
                    jnp.square(jnp.maximum(lower, 0.0))
                    + jnp.square(jnp.minimum(upper, 0.0))
                    + jnp.square(jnp.maximum(back, 0.0))
                    + jnp.square(jnp.minimum(side, 0.0))
                )
                crowding = jnp.concatenate([crowd[i, :, cut(block)]] * (grid_v // 8), 0)
                now[i, a, :, cut(block)] = (
                    centre
                    + pace * (x_row(block) - centre)
                    + slope[...] * (shifted(val, i, a, block, -1) - centre)
                    - (0.5 * CONTROL_COST) * bend
                    + VISCOSITY * (upper - lower + side - back)
                    + crowding
                )

        def density_row(i, a, x_row, up_row, down_row, up_now, down_now):
            pace = speed(a)
            for block in range(blocks):
                centre = den[i, a, :, cut(block)]
                control = now[i, a, :, cut(block)]
                above = up_row(block, centre)
                below = down_row(block, centre)
                rise = -CONTROL_COST * (up_now(block, control) - control)
                fall = -CONTROL_COST * (control - down_now(block, control))
                flux_up = jnp.maximum(rise, 0.0) * centre + jnp.minimum(rise, 0.0) * above
                flux_dn = jnp.maximum(fall, 0.0) * below + jnp.minimum(fall, 0.0) * centre
                right = pltpu.roll(centre, grid_v - 1, 0)
                turn = -CONTROL_COST * (pltpu.roll(control, grid_v - 1, 0) - control)
                flux_side = jnp.maximum(turn, 0.0) * centre + jnp.minimum(turn, 0.0) * right
                flux_side = jnp.where(last_b, 0.0, flux_side - VISCOSITY * (right - centre))
                flux_back = jnp.where(first_b, 0.0, pltpu.roll(flux_side, 1, 0))
                nxt[i, a, :, cut(block)] = (
                    centre
                    + pace * (x_row(block) - centre)
                    + slope[...] * (shifted(den, i, a, block, 1) - centre)
                    - (flux_up - flux_dn)
                    - (flux_side - flux_back)
                    + VISCOSITY * (above + below - 2.0 * centre)
                )

        def row_of(ref, i, a):
            return lambda block, centre=None: ref[i, a, :, cut(block)]

        def line_of(ref, a):
            return lambda block: ref[a, :, cut(block)]

        def edge_of(ref, side, i):
            clamp = vel == (0 if side == 0 else vels - 1)
            return lambda block, centre: jnp.where(clamp, centre, ref[side, i, :, cut(block)])

        def neighbours(ref, held, i, a, kind):
            up = edge_of(held, 1, i) if kind == "last" else row_of(ref, i, a + 1)
            down = edge_of(held, 0, i) if kind == "first" else row_of(ref, i, a - 1)
            return up, down

        def near_value(a, kind="middle"):
            value_row(near, a, row_of(val, far, a), *neighbours(val, val_h, near, a, kind))

        def far_value(a, kind="middle"):
            value_row(far, a, line_of(val_x, a), *neighbours(val, val_h, far, a, kind))

        def near_density(a, kind="middle"):
            density_row(
                near, a, line_of(den_x, a), *neighbours(den, den_h, near, a, kind),
                *neighbours(now, now_h, near, a, kind),
            )

        def far_density(a, kind="middle"):
            density_row(
                far, a, row_of(den, near, a), *neighbours(den, den_h, far, a, kind),
                *neighbours(now, now_h, far, a, kind),
            )

        def n_copies(i):
            return (
                remote(now.at[i, rows - 1], now_h.at[0, i], n_send.at[0, i], n_recv.at[0, i], upward),
                remote(now.at[i, 0], now_h.at[1, i], n_send.at[1, i], n_recv.at[1, i], downward),
            )

        def send_now(i):
            up, down = n_copies(i)
            pl.when(vel < vels - 1)(up.start)
            pl.when(vel > 0)(down.start)

        def loop(start, stop, step):
            def one(a, carry):
                step(a)
                return carry

            lax.fori_loop(start, stop, one, 0)

        def wait_x(which, a):
            x_copies(a)[which].wait_recv()

        def arrive(copies):
            up, down = copies
            pl.when(vel > 0)(up.wait_recv)
            pl.when(vel < vels - 1)(down.wait_recv)

        def advance(a):
            wait_x(0, a)
            far_value(a)

        def settle(a):
            advance(a)
            far_density(a - 1)
            wait_x(1, a)
            near_density(a)

        loop(1, rows - 1, near_value)
        loop(1, 3, advance)
        wait_x(1, 1)
        wait_x(1, 2)
        near_density(2)
        loop(3, 6, settle)
        arrive(h_copies(0))
        near_value(0, "first")
        near_value(rows - 1, "last")
        send_now(near)
        wait_x(0, 0)
        wait_x(0, rows - 1)
        far_value(0, "first")
        far_value(rows - 1, "last")
        send_now(far)
        loop(6, 12, settle)
        arrive(h_copies(1))
        for i in range(2):
            arrive(n_copies(i))
        near_density(1)
        far_density(1)
        wait_x(1, 0)
        near_density(0, "first")
        far_density(0, "first")
        wait_x(1, rows - 1)
        near_density(rows - 1, "last")
        loop(12, rows - 1, settle)
        far_density(rows - 2)
        far_density(rows - 1, "last")

        def drain(a):
            for copy in x_copies(a):
                copy.wait_send()

        loop(0, rows, drain)
        for which in (0, 1):
            up, down = h_copies(which)
            pl.when(vel < vels - 1)(up.wait_send)
            pl.when(vel > 0)(down.wait_send)
            up, down = n_copies(which)
            pl.when(vel < vels - 1)(up.wait_send)
            pl.when(vel > 0)(down.wait_send)
        for step in range(1, vels):
            m_copy(step).wait_send()

    return kernel


def solution(mesh):
    axes = mesh.axis_names
    vels, slabs = mesh.shape["vel"], mesh.shape["pos"]

    def body(value_next, density):
        depth, rows, grid_v, cells = value_next.shape
        line = (grid_v, cells)
        f32 = jnp.float32
        anywhere = pl.BlockSpec(memory_space=pltpu.HBM)
        held = pl.BlockSpec(memory_space=pltpu.VMEM)
        dma = pltpu.SemaphoreType.DMA
        return pl.pallas_call(
            make_kernel(vels, slabs, rows, grid_v, cells, axes),
            name="game_step",
            out_shape=(jax.ShapeDtypeStruct(value_next.shape, f32),) * 2,
            in_specs=[anywhere, anywhere],
            out_specs=(held, held),
            scratch_shapes=[
                pltpu.VMEM(value_next.shape, f32),
                pltpu.VMEM(value_next.shape, f32),
                pltpu.VMEM((rows,) + line, f32),
                pltpu.VMEM((rows,) + line, f32),
                pltpu.VMEM((2, depth) + line, f32),
                pltpu.VMEM((2, depth) + line, f32),
                pltpu.VMEM((2, depth) + line, f32),
                pltpu.VMEM((vels, 8, cells), f32),
                pltpu.VMEM((depth, 8, cells), f32),
                pltpu.VMEM((grid_v, LANES), f32),
                dma((2,)),
                dma((2, rows)),
                dma((2, rows)),
                dma((2, 2)),
                dma((2, 2)),
                dma((2, 2)),
                dma((2, 2)),
                dma((vels - 1,)),
                dma((vels - 1,)),
            ],
            compiler_params=pltpu.CompilerParams(
                collective_id=0, has_side_effects=True, vmem_limit_bytes=44 << 20
            ),
        )(value_next, density)

    spec = P("pos", "vel", None, None)
    return jax.shard_map(body, mesh=mesh, in_specs=(spec, spec), out_specs=(spec, spec), check_vma=False)
```

time: 189 us -> 70 us (0.37)
  the two profiles are of different devices: /device:TPU:7 before, /device:TPU:113 now
where the time goes in v1:
time: 70 us; the launch traced here: 69.9 us
  Pallas kernels  65.2 us (93%)
  local copies, waits for them, and re-layouts  4.03 us (6%)
    pallas_call x1, Pallas kernels, body(): pl.pallas_call(make_kernel(vels, slabs, rows, grid_v, cells, axes), name=...  65.2 us
    unnamed x2, local copies, waits for them, and re-layouts  4.03 us

profile of v1, /device:TPU:113, one launch (start us, length us, event | category | flops | bytes accessed | tf_op | source)
XLA Modules:
  0.0 69.9 jit_solution(13743164372615011264)
XLA Ops:
  0.6 65.2 %game_step.1 = (f32[2,16,64,512]{3,2,1,0:T(8,128)S(1)}, f32[2,16,64,512]{3,2,1,0:T(8,128)S(1)}) custom-call(f32[2,16,64,512]{3,2,1,0:T(8,128)} %value.1, f32[2,16,64,512]{3,2,1,0:T(8,128)} %density.1), custom_call_target="tpu_custom_call" | custom-call | tf_op jit(solution)/shard_map/game_step/pallas_call | solution.py:328
  65.9 2.0 %copy.6 = f32[2,16,64,512]{3,2,1,0:T(8,128)} copy(f32[2,16,64,512]{3,2,1,0:T(8,128)S(1)} %get-tuple-element.4) | data formatting | bytes 8388608
  67.9 2.0 %copy.7 = f32[2,16,64,512]{3,2,1,0:T(8,128)} copy(f32[2,16,64,512]{3,2,1,0:T(8,128)S(1)} %get-tuple-element.5) | data formatting | bytes 8388608
